TPU v7x, 32 devices: a whole 2x2x4 slice. The times are simulated.
32 devices in a mesh: pert: 2 (over y), ga: 4 (over z), band: 4 (over x, core).
Axes of the slice: x: 2, y: 2, z: 4, core: 2. Of those that a mesh axis runs over, the one named last changes fastest.
Arguments:
- psi: float32 [2, 4, 131072], P(None, 'band', 'ga'), may hold values from -6 to 6
- potential: float32 [256, 128, 128], P('pert', 'ga'), parts along dimension 0, may hold values from 1 to 3
- miller: int32 [131072], replicated, may hold values from 0 to 2097151, as said below
- occupied: int32 [4], replicated, may hold values 0 or 1
Outputs:
- projected: float32 [2, 8, 131072], P(None, ('pert', 'band'), 'ga'), parts along dimension 1
There are 2 independent parts, one for each index of `pert`. A program takes and returns all parts, laid end to end along the dimension named above; an argument that names none is the same for every part. Nothing has to cross between parts.
Inputs may be any that keep to these rules, and one draw needn't show every extreme that they name: `miller`: entry k is the flat index a 128^2 + b * 128 + c of coefficient k, with Fourier indices a, b, c in 0..127 taken modulo 128; the entries are distinct; each of a, b, c, read as a signed index in -64..128/2-1, lies in -32..128/4-1; the j-th block of 32768 entries holds only points whose signed a plus 128/4 is congruent to j modulo 131072/32768.
All inputs are finite; a program needn't handle non-finite values.
Results may differ from a plain program's by a relative error of at most 0.00013.
Values sent between devices are 32-bit elements; how exact they have to be, the bound alone decides.
A program may use at most 64 MiB of HBM per device.

v0:
```python
import jax
import jax.numpy as jnp
from jax import lax
from jax.sharding import PartitionSpec as P

NPW = 131072


highest = lax.Precision.HIGHEST


def phases(first_index, second_index, direction, length):
    turns = first_index[:, None] * second_index[None, :] % length
    angle = direction * 2.0 * jnp.pi / length * turns.astype(jnp.float32)
    return (jnp.cos(angle), jnp.sin(angle))


def contract(pattern, real_part, imag_part, twiddle):
    cosine, sine_part = twiddle
    out_real = jnp.einsum(pattern, real_part, cosine, precision=highest) - jnp.einsum(
        pattern, imag_part, sine_part, precision=highest
    )
    out_imag = jnp.einsum(pattern, real_part, sine_part, precision=highest) + jnp.einsum(
        pattern, imag_part, cosine, precision=highest
    )
    return (out_real, out_imag)


def inner_products(left_real, left_imag, right_real, right_imag):
    over_real = jnp.einsum("mk,nk->mn", left_real, right_real, precision=highest) + jnp.einsum(
        "mk,nk->mn", left_imag, right_imag, precision=highest
    )
    over_imag = jnp.einsum("mk,nk->mn", left_real, right_imag, precision=highest) - jnp.einsum(
        "mk,nk->mn", left_imag, right_real, precision=highest
    )
    return (over_real, over_imag)


def subtract(applied_real, applied_imag, basis_real, basis_imag, weight_real, weight_imag):
    proj_real = jnp.einsum("mn,mk->nk", weight_real, basis_real, precision=highest) - jnp.einsum(
        "mn,mk->nk", weight_imag, basis_imag, precision=highest
    )
    proj_imag = jnp.einsum("mn,mk->nk", weight_imag, basis_real, precision=highest) + jnp.einsum(
        "mn,mk->nk", weight_real, basis_imag, precision=highest
    )
    return (applied_real - proj_real, applied_imag - proj_imag)


def shards(psi, potential, miller, occupied):
    grid_size = potential.shape[0]
    owners = lax.axis_size("ga")
    quarter = grid_size // 4
    per_shard = psi.shape[2]
    band_count = psi.shape[1]
    owner_index = lax.axis_index("ga")
    kept_rows = grid_size // 2
    kept_planes = grid_size // (2 * owners)
    full_index = jnp.arange(grid_size, dtype=jnp.int32)
    kept_index = (jnp.arange(kept_rows, dtype=jnp.int32) + grid_size - quarter) % grid_size
    inverse_rows = phases(kept_index, full_index, 1.0, grid_size)
    forward_rows = phases(full_index, kept_index, -1.0, grid_size)
    slot_index = jnp.arange(owners * kept_planes, dtype=jnp.int32)
    plane_index = (
        slot_index // kept_planes + owners * (slot_index % kept_planes) + grid_size - quarter
    ) % grid_size
    inverse_planes = phases(plane_index, full_index, 1.0, grid_size)
    forward_planes = phases(full_index, plane_index, -1.0, grid_size)
    local_points = lax.dynamic_slice_in_dim(miller, owner_index * per_shard, per_shard)
    index_a = local_points // (grid_size * grid_size)
    index_b = local_points // grid_size % grid_size
    index_c = local_points % grid_size
    plane_pos = (index_a + quarter) % grid_size
    position = (plane_pos // owners * kept_rows + (index_b + quarter) % grid_size) * kept_rows + (
        index_c + quarter
    ) % grid_size
    slab_size = kept_planes * kept_rows * kept_rows
    real_part = jnp.zeros((band_count, slab_size), jnp.float32).at[:, position].set(psi[0])
    imag_part = jnp.zeros((band_count, slab_size), jnp.float32).at[:, position].set(psi[1])
    real_part = real_part.reshape(band_count, kept_planes, kept_rows, kept_rows)
    imag_part = imag_part.reshape(band_count, kept_planes, kept_rows, kept_rows)
    real_part, imag_part = contract("ntbc,by->ntyc", real_part, imag_part, inverse_rows)
    pieces = (
        lax.all_to_all(real_part, "ga", split_axis=2, concat_axis=1, tiled=True),
        lax.all_to_all(imag_part, "ga", split_axis=2, concat_axis=1, tiled=True),
    )
    wide_real, wide_imag = contract("nsyc,cz->nsyz", pieces[0], pieces[1], inverse_rows)
    pieces = (wide_real, wide_imag)
    wave_real, wave_imag = contract("nsyz,sx->nxyz", pieces[0], pieces[1], inverse_planes)
    wave_real = wave_real * potential
    wave_imag = wave_imag * potential
    wide_real, wide_imag = contract("nxyz,xs->nsyz", wave_real, wave_imag, forward_planes)
    narrow = contract("nsyz,zc->nsyc", wide_real, wide_imag, forward_rows)
    real_part = lax.all_to_all(narrow[0], "ga", split_axis=1, concat_axis=2, tiled=True)
    imag_part = lax.all_to_all(narrow[1], "ga", split_axis=1, concat_axis=2, tiled=True)
    real_part, imag_part = contract("ntyc,yb->ntbc", real_part, imag_part, forward_rows)
    inverse_volume = 1.0 / grid_size**3
    applied_real = real_part.reshape(band_count, slab_size)[:, position] * inverse_volume
    applied_imag = imag_part.reshape(band_count, slab_size)[:, position] * inverse_volume
    weights = occupied.astype(jnp.float32)[:, None]
    moved_parts = (
        lax.all_to_all(applied_real, "band", split_axis=1, concat_axis=0, tiled=True),
        lax.all_to_all(applied_imag, "band", split_axis=1, concat_axis=0, tiled=True),
        lax.all_to_all(psi[0], "band", split_axis=1, concat_axis=0, tiled=True),
        lax.all_to_all(psi[1], "band", split_axis=1, concat_axis=0, tiled=True),
    )
    column_real, column_imag, basis_real, basis_imag = moved_parts
    over_real, over_imag = inner_products(basis_real, basis_imag, column_real, column_imag)
    over_real, over_imag = lax.psum((over_real, over_imag), ("ga", "band"))
    weight_real = weights * (over_real / NPW)
    weight_imag = weights * (over_imag / NPW)
    left_real, left_imag = subtract(
        column_real, column_imag, basis_real, basis_imag, weight_real, weight_imag
    )
    left_real, left_imag = (
        lax.all_to_all(left_real, "band", split_axis=0, concat_axis=1, tiled=True),
        lax.all_to_all(left_imag, "band", split_axis=0, concat_axis=1, tiled=True),
    )
    return jnp.stack([left_real, left_imag])


def solution(mesh):
    in_specs = (P(None, "band", "ga"), P("pert", "ga", None), P(), P())
    out_specs = P(None, ("pert", "band"), "ga")
    return jax.shard_map(shards, mesh=mesh, in_specs=in_specs, out_specs=out_specs, check_vma=False)
```

profile of v0, /device:TPU:0, one launch (start us, length us, event | category | flops | bytes accessed | tf_op | source)
XLA Modules:
  0.0 796.1 jit_solution(8780782208961339326)
XLA Ops:
  3.1 120.4 %scatter_custom_fusion.1 = f32[65536]{0:T(1024)S(1)} fusion(s32[32768]{0:T(1024)S(1)} %get-tuple-element.8, f32[32768]{0:T(1024)} %bitcast.7, f32[]{:T(128)} %constant.167.clone.1), kind=kCustom, calls=%fused_computation.97 | custom fusion | bytes 262656 | tf_op jit(solution)/shard_map/scatter | solution.py:78
  123.8 120.4 %scatter_custom_fusion = f32[65536]{0:T(1024)S(1)} fusion(s32[32768]{0:T(1024)S(1)} %get-tuple-element.8, f32[32768]{0:T(1024)} %bitcast.3, f32[]{:T(128)} %constant.167.clone.1), kind=kCustom, calls=%fused_computation.99 | custom fusion | bytes 262656 | tf_op jit(solution)/shard_map/scatter | solution.py:77
  248.2 6.3 all-to-all-start
  258.1 10.9 %all-to-all-done = f32[4,1,32768]{2,1,0:T(1,128)S(1)} async-done(((f32[4,1,32768]{2,1,0:T(1,128)}), f32[4,1,32768]{2,1,0:T(1,128)S(1)}, u32[]{:S(2)}, u32[]{:S(2)}) %all-to-all-start) | async-done | bytes 524320 | tf_op jit(solution)/shard_map/all_to_all | solution.py:83
  269.0 3.9 all-to-all-start.1
  279.0 7.5 all-to-all-done.1
  299.5 3.6 subtract_multiply_fusion
  305.9 3.6 add_multiply_fusion
  317.9 3.5 all-to-all-start.2
  326.4 9.0 %all-to-all-done.2 = f32[4,1,32768]{2,1,0:T(1,128)S(1)} async-done(((f32[4,1,32768]{2,1,0:T(1,128)}), f32[4,1,32768]{2,1,0:T(1,128)S(1)}, u32[]{:S(2)}, u32[]{:S(2)}) %all-to-all-start.2) | async-done | bytes 524320 | tf_op jit(solution)/shard_map/all_to_all | solution.py:93
  335.4 3.6 all-to-all-start.3
  343.6 9.4 %all-to-all-done.3 = f32[4,1,32768]{2,1,0:T(1,128)S(1)} async-done(((f32[4,1,32768]{2,1,0:T(1,128)}), f32[4,1,32768]{2,1,0:T(1,128)S(1)}, u32[]{:S(2)}, u32[]{:S(2)}) %all-to-all-start.3) | async-done | bytes 524320 | tf_op jit(solution)/shard_map/all_to_all | solution.py:94
  360.2 180.5 %gather_fusion = f32[32768]{0:T(1024)S(1)} fusion(f32[65536]{0:T(1024)S(1)} %reshape.289, s32[32768]{0:T(1024)S(1)} %get-tuple-element.7), kind=kCustom, calls=%fused_computation | custom fusion | bytes 393216 | tf_op jit(solution)/shard_map/gather | solution.py:97
  542.4 180.5 %gather_fusion.1 = f32[32768]{0:T(1024)S(1)} fusion(f32[65536]{0:T(1024)S(1)} %reshape.299, s32[32768]{0:T(1024)S(1)} %get-tuple-element.7), kind=kCustom, calls=%fused_computation.1 | custom fusion | bytes 393216 | tf_op jit(solution)/shard_map/gather | solution.py:98
  723.0 3.3 all-to-all-start.4
  727.0 3.9 all-to-all-done.4
  730.9 3.3 all-to-all-start.6
  734.9 3.9 all-to-all-done.6
  738.8 3.3 all-to-all-start.7
  742.8 3.9 all-to-all-done.7
  748.2 30.3 %all-reduce = (f32[4,4]{0,1:T(4,128)S(1)}, f32[4,4]{0,1:T(4,128)S(1)}) all-reduce(f32[4,4]{0,1:T(4,128)S(1)} %fusion.8, f32[4,4]{0,1:T(4,128)S(1)} %fusion.9), channel_id=1, replica_groups=mesh['pert'=2,'ga'=4,'band'=4] {'ga','band'}, use_global_device_ids=true, to_apply=%region_3.4 | all-reduce | flops 32 | bytes 256 | tf_op jit(solution)/shard_map/psum | solution.py:108
  780.1 3.3 all-to-all-start.8
  784.5 3.5 all-to-all-done.8
  788.0 7.0 all_to_all.144
  (75 shorter events, 66.4 us)
Async XLA Ops:
  248.2 20.8 %all-to-all-start = ((f32[4,1,32768]{2,1,0:T(1,128)}), f32[4,1,32768]{2,1,0:T(1,128)S(1)}, u32[]{:S(2)}, u32[]{:S(2)}) async-start(f32[4,1,32768]{2,1,0:T(1,128)} %reshape.365), calls=%async_computation | async-start | bytes 1048576 | tf_op jit(solution)/shard_map/all_to_all | solution.py:83
  269.0 17.5 %all-to-all-start.1 = ((f32[4,1,32768]{2,1,0:T(1,128)}), f32[4,1,32768]{2,1,0:T(1,128)S(1)}, u32[]{:S(2)}, u32[]{:S(2)}) async-start(f32[4,1,32768]{2,1,0:T(1,128)} %reshape.367), calls=%async_computation.1 | async-start | bytes 1048576 | tf_op jit(solution)/shard_map/all_to_all | solution.py:84
  297.9 1.6 copy-start
  317.9 17.5 %all-to-all-start.2 = ((f32[4,1,32768]{2,1,0:T(1,128)}), f32[4,1,32768]{2,1,0:T(1,128)S(1)}, u32[]{:S(2)}, u32[]{:S(2)}) async-start(f32[4,1,32768]{2,1,0:T(1,128)} %reshape.369), calls=%async_computation.2 | async-start | bytes 1048576 | tf_op jit(solution)/shard_map/all_to_all | solution.py:93
  335.4 17.6 %all-to-all-start.3 = ((f32[4,1,32768]{2,1,0:T(1,128)}), f32[4,1,32768]{2,1,0:T(1,128)S(1)}, u32[]{:S(2)}, u32[]{:S(2)}) async-start(f32[4,1,32768]{2,1,0:T(1,128)} %reshape.371), calls=%async_computation.3 | async-start | bytes 1048576 | tf_op jit(solution)/shard_map/all_to_all | solution.py:94
  353.0 369.9 %all-to-all-start.5 = ((f32[1,4,8192]{2,0,1:T(1,128)}), f32[1,4,8192]{2,0,1:T(1,128)S(1)}, u32[]{:S(2)}, u32[]{:S(2)}) async-start(f32[1,4,8192]{2,0,1:T(1,128)} %bitcast.45), calls=%async_computation.5 | async-start | bytes 262144 | tf_op jit(solution)/shard_map/all_to_all | solution.py:103
  723.0 25.2 %copy-start.1 = (s32[4]{0:T(128)S(1)}, s32[4]{0:T(128)}, u32[]{:S(2)}) copy-start(s32[4]{0:T(128)} %param.7) | copy-start | bytes 52
  723.0 7.9 all-to-all-start.4
  730.9 7.9 all-to-all-start.6
  738.8 7.9 all-to-all-start.7
  780.1 7.9 all-to-all-start.8
where the time goes:
time: 803 us; the launch traced here: 796 us
  local copies, waits for them, and re-layouts  617 us (77%)
  waiting for transfers between devices  51.9 us (6%)
  matrix products  41.5 us (5%)
  blocking collectives  37.3 us (5%)
  starting transfers between devices  34 us (4%)
  other arithmetic  13.3 us (2%)
    gather x1, local copies, waits for them, and re-layouts, shards(): real_part.reshape(band_count, slab_size)[:, position] * inverse_volume  181 us
    gather x1, local copies, waits for them, and re-layouts, shards(): imag_part.reshape(band_count, slab_size)[:, position] * inverse_volume  181 us
    scatter x1, local copies, waits for them, and re-layouts, shards(): jnp.zeros((band_count, slab_size), jnp.float32).at[:, position].set(psi[0])  120 us
    scatter x1, local copies, waits for them, and re-layouts, shards(): jnp.zeros((band_count, slab_size), jnp.float32).at[:, position].set(psi[1])  120 us
    psum x1, blocking collectives, shards(): over_real, over_imag = lax.psum((over_real, over_imag), ('ga', 'band'))  30.3 us
  transfers between devices with their start and end apart: 9, of which 8 were waited for; matrix products, arithmetic and copies ran while one was open for 49% of the time, Pallas kernels for 0%

commit v1 on v0

--- a/solution.py
+++ b/solution.py
@@ -1,9 +1,270 @@
+import functools
+
 import jax
 import jax.numpy as jnp
+import numpy as np
 from jax import lax
+from jax.experimental import pallas as pl
+from jax.experimental.pallas import tpu as pltpu
 from jax.sharding import PartitionSpec as P
 
-NPW = 131072
+F32 = jnp.float32
+BF16 = jnp.bfloat16
+CHUNK = 2048
+ROWS = 8
+
+
+def halves(value):
+    high = value.astype(BF16)
+    return high, (value - high.astype(F32)).astype(BF16)
+
+
+def const_halves(value):
+    value = np.asarray(value, np.float32)
+    high = value.astype(BF16)
+    return high, (value - high.astype(np.float32)).astype(BF16)
+
+
+def left_const(value):
+    high, low = const_halves(value)
+    return jnp.asarray(np.concatenate([high, high, low], axis=1))
+
+
+def right_const(value):
+    high, low = const_halves(value)
+    return jnp.asarray(np.concatenate([high, high, low], axis=0))
+
+
+def left_mul(weights, value):
+    high, low = halves(value)
+    return jnp.dot(weights, jnp.concatenate([high, low, high], axis=0), preferred_element_type=F32)
+
+
+def right_mul(value, weights):
+    high, low = halves(value)
+    return jnp.dot(jnp.concatenate([high, low, high], axis=1), weights, preferred_element_type=F32)
+
+
+def turn(value, kept):
+    groups = []
+    for start in range(0, value.shape[1], 2 * kept):
+        groups.append(-value[:, start + kept : start + 2 * kept])
+        groups.append(value[:, start : start + kept])
+    return jnp.concatenate(groups, axis=1)
+
+
+class Sizes:
+    def __init__(self, psi, potential, owners):
+        self.n = potential.shape[0]
+        self.owners = owners
+        self.kept = self.n // 2
+        self.planes = self.n // (2 * owners)
+        self.inner = min(4, self.planes)
+        self.outer = self.planes // self.inner
+        self.block = self.n // owners
+        self.points = psi.shape[2]
+        self.bands = psi.shape[1]
+        self.rows = self.outer * self.kept
+        self.lanes = self.inner * 2 * self.kept
+        self.chunk = min(CHUNK, self.points)
+
+
+def twiddles(s):
+    n, kept, quarter = s.n, s.kept, s.n // 4
+    full = np.arange(n)
+    signed = np.arange(kept) - quarter
+    angle = 2.0 * np.pi / n * ((signed[:, None] * full[None, :]) % n)
+    cosine, sine = np.cos(angle), np.sin(angle)
+    rows_in = np.concatenate([cosine.T, sine.T], axis=1)
+    rows_out = np.concatenate([cosine, -sine], axis=1) / float(n) ** 3
+    z_in = np.block([[cosine, sine], [-sine, cosine]])
+    z_out = np.block([[cosine.T, -sine.T], [sine.T, cosine.T]])
+    inner, owner, outer = np.meshgrid(
+        np.arange(s.inner), np.arange(s.owners), np.arange(s.outer), indexing="ij"
+    )
+    plane = ((outer * s.inner + inner) * s.owners + owner).reshape(s.inner, -1)
+    cos_p, sin_p = cosine[plane], sine[plane]
+    real_row = np.stack([cos_p, -sin_p], axis=1).reshape(-1, n)
+    imag_row = np.stack([sin_p, cos_p], axis=1).reshape(-1, n)
+    x_in = np.concatenate([real_row, imag_row], axis=1).T
+    real_row = np.stack([cos_p, -sin_p], axis=1).reshape(-1, n)
+    imag_row = np.stack([sin_p, cos_p], axis=1).reshape(-1, n)
+    x_out = np.concatenate([real_row, imag_row], axis=1)
+    return {
+        "rows_in": left_const(rows_in),
+        "rows_out": left_const(rows_out),
+        "z_in": right_const(z_in),
+        "z_out": right_const(z_out),
+        "x_in": left_const(x_in),
+        "x_out": left_const(x_out),
+    }
+
+
+def spread_kernel(s, code_ref, psi_ref, iota_ref, weight_ref, out_ref, acc):
+    acc[...] = jnp.zeros_like(acc)
+
+    @pl.loop(0, s.points // s.chunk)
+    def _(step):
+        at = pl.ds(pl.multiple_of(step * s.chunk, s.chunk), s.chunk)
+        codes = code_ref[:, at].astype(BF16)
+        high, low = halves(psi_ref[:, at])
+        zero = jnp.zeros((), BF16)
+        row_hot = jnp.where(iota_ref[: s.rows, :] == codes[0:1], jnp.ones((), BF16), zero)
+        total = None
+        for part in (high, low):
+            pieces = []
+            for group in range(s.inner):
+                mask = iota_ref[group * s.kept : (group + 1) * s.kept, :] == codes[1:2]
+                for kind in range(2):
+                    pieces.append(jnp.where(mask, part[kind : kind + 1], zero))
+            value = jnp.concatenate(pieces, axis=0)
+            term = lax.dot_general(
+                row_hot, value, (((1,), (1,)), ((), ())), preferred_element_type=F32
+            )
+            total = term if total is None else total + term
+        acc[...] += total
+
+    for outer in range(s.outer):
+        field = acc[outer * s.kept : (outer + 1) * s.kept, :]
+        both = jnp.concatenate([field, turn(field, s.kept)], axis=0)
+        result = left_mul(weight_ref[...], both)
+        for owner in range(s.owners):
+            out_ref[owner, outer] = result[owner * s.block : (owner + 1) * s.block]
+
+
+def middle_kernel(s, in_ref, pot_ref, z_in, x_in, x_out, z_out, out_ref):
+    n = s.n
+    gt = s.owners * s.outer
+    width = 2 * s.kept
+    planes = []
+    for inner in range(s.inner):
+        value = in_ref[:, :, inner * width : (inner + 1) * width].reshape(gt * ROWS, width)
+        wide = right_mul(value, z_in[...])
+        for kind in range(2):
+            piece = wide[:, kind * n : (kind + 1) * n].reshape(gt, ROWS, n)
+            planes.append(jnp.swapaxes(piece, 0, 1))
+    columns = [
+        jnp.concatenate([piece[row] for piece in planes], axis=0) for row in range(ROWS)
+    ]
+    wave = left_mul(x_in[...], jnp.concatenate(columns, axis=1))
+    pot = jnp.swapaxes(pot_ref[...], 0, 1)
+    pot = jnp.concatenate([pot[row] for row in range(ROWS)], axis=1)
+    product = jnp.concatenate([wave[:n] * pot, wave[n:] * pot], axis=0)
+    back = left_mul(x_out[...], product)
+    for inner in range(s.inner):
+        kinds = []
+        for kind in range(2):
+            start = (inner * 2 + kind) * gt
+            piece = jnp.stack(
+                [back[start : start + gt, row * n : (row + 1) * n] for row in range(ROWS)]
+            )
+            kinds.append(jnp.swapaxes(piece, 0, 1).reshape(gt * ROWS, n))
+        narrow = right_mul(jnp.concatenate(kinds, axis=1), z_out[...])
+        out_ref[:, :, inner * width : (inner + 1) * width] = narrow.reshape(gt, ROWS, width)
+
+
+def pick_kernel(s, in_ref, code_ref, basis_ref, iota_ref, weight_ref, out_ref, over_ref, table):
+    for outer in range(s.outer):
+        rows = jnp.concatenate([in_ref[owner, outer] for owner in range(s.owners)], axis=0)
+        both = jnp.concatenate([rows, turn(rows, s.kept)], axis=0)
+        field = left_mul(weight_ref[...], both)
+        high, low = halves(field.T)
+        table[:, outer * s.kept : (outer + 1) * s.kept] = high
+        table[:, s.rows + outer * s.kept : s.rows + (outer + 1) * s.kept] = low
+    over_ref[...] = jnp.zeros_like(over_ref)
+
+    @pl.loop(0, s.points // s.chunk)
+    def _(step):
+        at = pl.ds(pl.multiple_of(step * s.chunk, s.chunk), s.chunk)
+        codes = code_ref[:, at].astype(BF16)
+        one_hot = jnp.where(iota_ref[: s.rows, :] == codes[0:1], jnp.ones((), BF16), jnp.zeros((), BF16))
+        found = jnp.dot(table[:, : s.rows], one_hot, preferred_element_type=F32) + jnp.dot(
+            table[:, s.rows :], one_hot, preferred_element_type=F32
+        )
+        lane = code_ref[1:2, at]
+        index = lax.broadcasted_iota(jnp.int32, (s.kept, s.chunk), 0).astype(F32)
+        sums = [None, None]
+        for group in range(s.inner):
+            mask = index == lane - float(group * s.kept)
+            for kind in range(2):
+                start = (group * 2 + kind) * s.kept
+                piece = jnp.where(mask, found[start : start + s.kept], 0.0)
+                sums[kind] = piece if sums[kind] is None else sums[kind] + piece
+        real = jnp.sum(sums[0], axis=0, keepdims=True)
+        imag = jnp.sum(sums[1], axis=0, keepdims=True)
+        out_ref[0:1, at] = real
+        out_ref[1:2, at] = imag
+        left_real = basis_ref[0, :, at]
+        left_imag = basis_ref[1, :, at]
+        over_ref[0] += left_real * real + left_imag * imag
+        over_ref[1] += left_real * imag - left_imag * real
+
+
+def local_codes(s, miller):
+    quarter = s.n // 4
+    points = lax.dynamic_slice_in_dim(miller, lax.axis_index("ga") * s.points, s.points)
+    slot = (points // (s.n * s.n) + quarter) % s.n // s.owners
+    row = (points // s.n + quarter) % s.n
+    column = (points + quarter) % s.n
+    high = slot // s.inner * s.kept + row
+    low = slot % s.inner * s.kept + column
+    return jnp.stack([high, low]).astype(F32)
+
+
+VMEM = pl.BlockSpec(memory_space=pltpu.VMEM)
+PARAMS = pltpu.CompilerParams(vmem_limit_bytes=56 * 1024 * 1024)
+
+
+def call(kernel, s, out, count, scratch=()):
+    return pl.pallas_call(
+        functools.partial(kernel, s),
+        out_shape=out,
+        in_specs=[VMEM] * count,
+        out_specs=jax.tree.map(lambda _: VMEM, out),
+        scratch_shapes=list(scratch),
+        compiler_params=PARAMS,
+    )
+
+
+def shards(psi, potential, miller, occupied):
+    s = Sizes(psi, potential, lax.axis_size("ga"))
+    w = twiddles(s)
+    shape = jax.ShapeDtypeStruct
+    basis = lax.all_gather(psi, "band", axis=1, tiled=True)
+    codes = local_codes(s, miller)
+    count = max(s.rows, s.inner * s.kept)
+    iota = lax.broadcasted_iota(jnp.int32, (count, s.chunk), 0).astype(BF16)
+    sent = call(
+        spread_kernel, s, shape((s.owners, s.outer, s.block, s.lanes), F32), 4,
+        [pltpu.VMEM((s.rows, s.lanes), F32)],
+    )(codes, psi[:, 0], iota, w["rows_in"])
+    got = lax.all_to_all(sent, "ga", split_axis=0, concat_axis=0, tiled=True)
+    gt = s.owners * s.outer
+    whole = [w["z_in"], w["x_in"], w["x_out"], w["z_out"]]
+    sent = pl.pallas_call(
+        functools.partial(middle_kernel, s),
+        out_shape=shape((gt, s.block, s.lanes), F32),
+        grid=(s.block // ROWS,),
+        in_specs=[
+            pl.BlockSpec((gt, ROWS, s.lanes), lambda i: (0, i, 0)),
+            pl.BlockSpec((s.n, ROWS, s.n), lambda i: (0, i, 0)),
+        ] + [pl.BlockSpec(v.shape, lambda i: (0, 0)) for v in whole],
+        out_specs=pl.BlockSpec((gt, ROWS, s.lanes), lambda i: (0, i, 0)),
+        compiler_params=PARAMS,
+    )(got.reshape(gt, s.block, s.lanes), potential, *whole)
+    sent = sent.reshape(s.owners, s.outer, s.block, s.lanes)
+    got = lax.all_to_all(sent, "ga", split_axis=0, concat_axis=0, tiled=True)
+    bands = basis.shape[1]
+    applied, over = call(
+        pick_kernel, s, (shape((2, s.points), F32), shape((2, bands, s.chunk), F32)), 5,
+        [pltpu.VMEM((s.lanes, 2 * s.rows), BF16)],
+    )(got, codes, basis, iota, w["rows_out"])
+    total = s.points * s.owners
+    over = lax.psum(jnp.sum(over, axis=2), "ga") / total * occupied.astype(F32)
+    real, imag = over[0][:, None], over[1][:, None]
+    proj_real = jnp.sum(basis[0] * real - basis[1] * imag, axis=0)
+    proj_imag = jnp.sum(basis[0] * imag + basis[1] * real, axis=0)
+    return jnp.stack([applied[0] - proj_real, applied[1] - proj_imag])[:, None]
 
 
 highest = lax.Precision.HIGHEST
@@ -46,12 +307,13 @@
     return (applied_real - proj_real, applied_imag - proj_imag)
 
 
-def shards(psi, potential, miller, occupied):
+def plain_shards(psi, potential, miller, occupied):
     grid_size = potential.shape[0]
     owners = lax.axis_size("ga")
     quarter = grid_size // 4
     per_shard = psi.shape[2]
     band_count = psi.shape[1]
+    total = per_shard * lax.axis_size("ga")
     owner_index = lax.axis_index("ga")
     kept_rows = grid_size // 2
     kept_planes = grid_size // (2 * owners)
@@ -106,8 +368,8 @@
     column_real, column_imag, basis_real, basis_imag = moved_parts
     over_real, over_imag = inner_products(basis_real, basis_imag, column_real, column_imag)
     over_real, over_imag = lax.psum((over_real, over_imag), ("ga", "band"))
-    weight_real = weights * (over_real / NPW)
-    weight_imag = weights * (over_imag / NPW)
+    weight_real = weights * (over_real / total)
+    weight_imag = weights * (over_imag / total)
     left_real, left_imag = subtract(
         column_real, column_imag, basis_real, basis_imag, weight_real, weight_imag
     )
@@ -119,6 +381,11 @@
 
 
 def solution(mesh):
+    def body(psi, potential, miller, occupied):
+        if potential.shape[1] % ROWS:
+            return plain_shards(psi, potential, miller, occupied)
+        return shards(psi, potential, miller, occupied)
+
     in_specs = (P(None, "band", "ga"), P("pert", "ga", None), P(), P())
     out_specs = P(None, ("pert", "band"), "ga")
-    return jax.shard_map(shards, mesh=mesh, in_specs=in_specs, out_specs=out_specs, check_vma=False)
+    return jax.shard_map(body, mesh=mesh, in_specs=in_specs, out_specs=out_specs, check_vma=False)

time: 803 us -> 155 us (0.19)
  local copies, waits for them, and re-layouts: 617 us -> 9.46 us
  Pallas kernels: 0 us -> 57.4 us
  matrix products: 41.5 us -> 0 us
  blocking collectives: 37.3 us -> 9.82 us
  starting transfers between devices: 34 us -> 10 us
  between operations: 0.7 us -> 13.5 us
    gather x2 -> x0, local copies, waits for them, and re-layouts: 361 us -> none  [the longest x1 181 us: shards(): real_part.reshape(band_count, slab_size)[:, position] * inverse_volume]
    scatter x2 -> x0, local copies, waits for them, and re-layouts: 241 us -> none  [the longest x1 120 us: shards(): jnp.zeros((band_count, slab_size), jnp.float32).at[:, position].set(psi[0])]
    pallas_call x0 -> x3, Pallas kernels: none -> 57.4 us  [the longest x1 25.5 us: shards(): call(pick_kernel, s, (shape((2, s.points), F32), shape((2, bands, s.chunk...]
    dot_general x28 -> x0, matrix products: 38.4 us -> none  [the longest x5 9.3 us: contract(): jnp.einsum(pattern, imag_part, cosine, precision=highest)]
    all_to_all x9 -> x2, starting transfers between devices: 34 us -> 9.99 us  [shards(): got = lax.all_to_all(sent, 'ga', split_axis=0, concat_axis=0, tiled=True)]
    psum x1, blocking collectives: 30.3 us -> 9.82 us  [shards(): over = lax.psum(jnp.sum(over, axis=2), 'ga') / total * occupied.astype(F32)]
    all_to_all x4 -> x0, other arithmetic: 9.52 us -> none  [the longest x1 2.98 us: shards(): lax.all_to_all(imag_part, 'ga', split_axis=2, concat_axis=1, tiled=True)]
    all_to_all x9 -> x2, waiting for transfers between devices: 51.9 us -> 47.3 us  [shards(): got = lax.all_to_all(sent, 'ga', split_axis=0, concat_axis=0, tiled=True)]
  transfers between devices with their start and end apart: 9 -> 3, of which waited for: 8 -> 2; matrix products, arithmetic and copies ran while one was open for 49% -> 2% of each run, Pallas kernels for 0% -> 5%
where the time goes in v1:
time: 155 us; the launch traced here: 154 us
  Pallas kernels  57.4 us (37%)
  waiting for transfers between devices  48 us (31%)
  between operations  13.5 us (9%)
  starting transfers between devices  10 us (6%)
  blocking collectives  9.82 us (6%)
  local copies, waits for them, and re-layouts  9.46 us (6%)
  other arithmetic  5.94 us (4%)
    all_to_all x2, waiting for transfers between devices, shards(): got = lax.all_to_all(sent, 'ga', split_axis=0, concat_axis=0, tiled=True)  47.3 us
    pallas_call x1, Pallas kernels, shards(): call(pick_kernel, s, (shape((2, s.points), F32), shape((2, bands, s.chunk...  25.5 us
    pallas_call x1, Pallas kernels, shards(): call(spread_kernel, s, shape((s.owners, s.outer, s.block, s.lanes), F32),...  24.1 us
    all_to_all x2, starting transfers between devices, shards(): got = lax.all_to_all(sent, 'ga', split_axis=0, concat_axis=0, tiled=True)  9.99 us
    psum x1, blocking collectives, shards(): over = lax.psum(jnp.sum(over, axis=2), 'ga') / total * occupied.astype(F32)  9.82 us
    pallas_call x1, Pallas kernels, shards(): pl.pallas_call(functools.partial(middle_kernel, s), out_shape=shape((gt,...  7.8 us
    unnamed x13, local copies, waits for them, and re-layouts  3.86 us
  transfers between devices with their start and end apart: 3, of which 2 were waited for; matrix products, arithmetic and copies ran while one was open for 2% of the time, Pallas kernels for 5%

profile of v1, /device:TPU:0, one launch (start us, length us, event | category | flops | bytes accessed | tf_op | source)
XLA Modules:
  0.0 154.1 jit_solution(3162761275889350941)
XLA Ops:
  6.5 1.3 fusion.9
  7.9 1.2 fusion.14
  9.1 1.9 %copy.22 = f32[2,1,32768]{2,0,1:T(2,128)} copy(f32[2,1,32768]{2,1,0:T(1,128)} %param.10) | data formatting | bytes 524288
  10.9 0.9 add_convert_fusion.code_ref
  11.8 1.2 iota.11.iota_ref
  13.0 24.1 %shard_map.100 = f32[4,4,32,512]{3,2,1,0:T(8,128)} custom-call(f32[2,32768]{1,0:T(2,128)} %add_convert_fusion.code_ref, f32[2,32768]{1,0:T(2,128)} %bitcast.34, bf16[256,2048]{1,0:T(8,128)(2,1)} %iota.11.iota_ref, bf16[128,384]{1,0:T(8,128)(2,1)} %constant.107.clone.weight_ref), custom_call_target="tpu_custom_call" | custom-call | tf_op jit(solution)/shard_map/pallas_call | solution.py:237
  37.1 6.3 %all-to-all-start = ((f32[4,4,32,512]{3,2,1,0:T(8,128)}), f32[4,4,32,512]{3,2,1,0:T(8,128)S(1)}, u32[]{:S(2)}, u32[]{:S(2)}) async-start(f32[4,4,32,512]{3,2,1,0:T(8,128)} %shard_map.100), calls=%async_computation | async-start | bytes 2097152 | tf_op jit(solution)/shard_map/all_to_all | solution.py:241
  43.4 0.7 all-gather.2.cloned.1.call-update
  44.1 25.0 %all-to-all-done = f32[4,4,32,512]{3,2,1,0:T(8,128)S(1)} async-done(((f32[4,4,32,512]{3,2,1,0:T(8,128)}), f32[4,4,32,512]{3,2,1,0:T(8,128)S(1)}, u32[]{:S(2)}, u32[]{:S(2)}) %all-to-all-start) | async-done | bytes 1048608 | tf_op jit(solution)/shard_map/all_to_all | solution.py:241
  69.2 1.0 copy-done.1
  70.2 7.8 %shard_map.101 = f32[16,32,512]{2,1,0:T(8,128)} custom-call(f32[16,32,512]{2,1,0:T(8,128)} %bitcast.32, f32[128,32,128]{2,1,0:T(8,128)} %pot_ref.1, bf16[384,256]{1,0:T(8,128)(2,1)} %constant.109.clone.z_in, bf16[256,384]{1,0:T(8,128)(2,1)} %constant.111.clone.x_in, bf16[128,768]{1,0:T(8,128)(2,1)} %constant.112.clone.x_out, ...), custom_call_target="tpu_custom_call" | custom-call | tf_op jit(solution)/shard_map/pallas_call | solution.py:244
  78.0 3.6 %all-to-all-start.1 = ((f32[4,4,32,512]{3,2,1,0:T(8,128)}), f32[4,4,32,512]{3,2,1,0:T(8,128)S(1)}, u32[]{:S(2)}, u32[]{:S(2)}) async-start(f32[4,4,32,512]{3,2,1,0:T(8,128)} %bitcast.33), calls=%async_computation.1 | async-start | bytes 2097152 | tf_op jit(solution)/shard_map/all_to_all | solution.py:256
  81.6 0.0 all-gather.2.cloned.1.call-done
  81.7 2.9 %copy.13.basis_ref = f32[2,4,32768]{2,1,0:T(4,128)} copy(f32[2,4,32768]{2,0,1:T(2,128)} %all-gather.2.cloned.1.call-done) | data formatting | bytes 2097152 | tf_op jit(solution)/shard_map/all_gather | solution.py:233
  84.6 22.3 %all-to-all-done.1.in_ref = f32[4,4,32,512]{3,2,1,0:T(8,128)S(1)} async-done(((f32[4,4,32,512]{3,2,1,0:T(8,128)}), f32[4,4,32,512]{3,2,1,0:T(8,128)S(1)}, u32[]{:S(2)}, u32[]{:S(2)}) %all-to-all-start.1) | async-done | bytes 1048608 | tf_op jit(solution)/shard_map/all_to_all | solution.py:256
  106.9 1.0 copy-done.2
  107.8 25.5 %shard_map.102 = (f32[2,32768]{1,0:T(2,128)}, f32[2,4,2048]{2,1,0:T(4,128)}) custom-call(f32[4,4,32,512]{3,2,1,0:T(8,128)} %copy-done.2, f32[2,32768]{1,0:T(2,128)} %add_convert_fusion.code_ref, f32[2,4,32768]{2,1,0:T(4,128)} %copy.13.basis_ref, bf16[256,2048]{1,0:T(8,128)(2,1)} %iota.11.iota_ref, bf16[64,768]{1,0:T(8,128)(2,1)} %constant.108.clone.weight_ref), custom_call_target="tpu_custom_call" | custom-call | tf_op jit(solution)/shard_map/pallas_call | solution.py:258
  133.4 1.0 reduce_sum.31
  134.4 0.5 slice.27
  134.9 9.8 %psum.7 = f32[2,4]{1,0:T(2,128)S(1)} all-reduce(f32[2,4]{1,0:T(2,128)S(1)} %reduce_sum.31), channel_id=1, replica_groups=mesh['pert'=2,'ga'=4,'band'=4] {'ga'}, use_global_device_ids=true, to_apply=%region_1.2 | all-reduce | flops 8 | bytes 64 | tf_op jit(solution)/shard_map/psum | solution.py:263
  144.8 0.9 fusion.1
  145.7 0.3 slice_subtract_fusion.1
  146.0 0.2 maximum_bitcast_fusion
  146.3 1.0 copy.15
  (15 shorter events, 0.0 us)
Async XLA Ops:
  37.1 32.1 %all-to-all-start = ((f32[4,4,32,512]{3,2,1,0:T(8,128)}), f32[4,4,32,512]{3,2,1,0:T(8,128)S(1)}, u32[]{:S(2)}, u32[]{:S(2)}) async-start(f32[4,4,32,512]{3,2,1,0:T(8,128)} %shard_map.100), calls=%async_computation | async-start | bytes 2097152 | tf_op jit(solution)/shard_map/all_to_all | solution.py:241
  43.4 38.2 %all-gather.2.cloned.1.call-start = ((), (), s32[]{:S(2)}) async-start(), calls=%async_computation.2 | async-start | bytes 1310720 | tf_op jit(solution)/shard_map/all_gather | solution.py:233
  69.2 1.0 copy-start.1
  78.0 3.7 %copy-start.5 = (s32[4]{0:T(128)S(1)}, s32[4]{0:T(128)}, u32[]{:S(2)}) copy-start(s32[4]{0:T(128)} %param.13) | copy-start | bytes 52
  78.0 28.9 %all-to-all-start.1 = ((f32[4,4,32,512]{3,2,1,0:T(8,128)}), f32[4,4,32,512]{3,2,1,0:T(8,128)S(1)}, u32[]{:S(2)}, u32[]{:S(2)}) async-start(f32[4,4,32,512]{3,2,1,0:T(8,128)} %bitcast.33), calls=%async_computation.1 | async-start | bytes 2097152 | tf_op jit(solution)/shard_map/all_to_all | solution.py:256
  84.6 49.8 %copy-start.3 = (f32[2,4,32768]{2,0,1:T(2,128)S(1)}, f32[2,4,32768]{2,0,1:T(2,128)}, u32[]{:S(2)}) copy-start(f32[2,4,32768]{2,0,1:T(2,128)} %all-gather.2.cloned.1.call-done) | copy-start | bytes 3145732
  84.6 60.2 %copy-start = (f32[2,4,32768]{2,1,0:T(4,128)S(1)}, f32[2,4,32768]{2,1,0:T(4,128)}, u32[]{:S(2)}) copy-start(f32[2,4,32768]{2,1,0:T(4,128)} %copy.13.basis_ref) | copy-start | bytes 3145732
  106.9 1.0 copy-start.2
  133.4 12.3 %copy-start.4 = (f32[2,32768]{1,0:T(2,128)S(1)}, f32[2,32768]{1,0:T(2,128)}, u32[]{:S(2)}) copy-start(f32[2,32768]{1,0:T(2,128)} %get-tuple-element.7) | copy-start | bytes 786436
Sparse Core Ops, SparseCore 0:
  45.8 18.1 all-gather.1

commit v2 on v1

--- a/solution.py
+++ b/solution.py
@@ -11,6 +11,8 @@
 F32 = jnp.float32
 BF16 = jnp.bfloat16
 CHUNK = 2048
+LANES = 128
+MESH = pl.DeviceIdType.MESH
 ROWS = 8
 
 
@@ -67,6 +69,10 @@
         self.rows = self.outer * self.kept
         self.lanes = self.inner * 2 * self.kept
         self.chunk = min(CHUNK, self.points)
+        self.lines = self.chunk // LANES
+        self.parts = 2 if self.inner % 2 == 0 else 1
+        self.groups = self.inner // self.parts
+        self.width = self.groups * 2 * self.kept
 
 
 def twiddles(s):
@@ -100,45 +106,125 @@
     }
 
 
-def spread_kernel(s, code_ref, psi_ref, iota_ref, weight_ref, out_ref, acc):
-    acc[...] = jnp.zeros_like(acc)
-
-    @pl.loop(0, s.points // s.chunk)
-    def _(step):
-        at = pl.ds(pl.multiple_of(step * s.chunk, s.chunk), s.chunk)
-        codes = code_ref[:, at].astype(BF16)
-        high, low = halves(psi_ref[:, at])
-        zero = jnp.zeros((), BF16)
-        row_hot = jnp.where(iota_ref[: s.rows, :] == codes[0:1], jnp.ones((), BF16), zero)
-        total = None
-        for part in (high, low):
-            pieces = []
-            for group in range(s.inner):
-                mask = iota_ref[group * s.kept : (group + 1) * s.kept, :] == codes[1:2]
-                for kind in range(2):
-                    pieces.append(jnp.where(mask, part[kind : kind + 1], zero))
-            value = jnp.concatenate(pieces, axis=0)
-            term = lax.dot_general(
-                row_hot, value, (((1,), (1,)), ((), ())), preferred_element_type=F32
+def meet(axes):
+    barrier = pltpu.get_barrier_semaphore()
+    for axis in axes:
+        size = lax.axis_size(axis)
+        for step in range(1, size):
+            peer = lax.rem(lax.axis_index(axis) + step, size)
+            pl.semaphore_signal(barrier, inc=1, device_id={axis: peer}, device_id_type=MESH)
+    pl.semaphore_wait(barrier, sum(lax.axis_size(axis) - 1 for axis in axes))
+
+
+def to_peer(axis, step, source, target, send_sem, recv_sem):
+    size = lax.axis_size(axis)
+    peer = lax.rem(lax.axis_index(axis) + step, size)
+    return pltpu.make_async_remote_copy(
+        src_ref=source,
+        dst_ref=target,
+        send_sem=send_sem,
+        recv_sem=recv_sem,
+        device_id={axis: peer},
+        device_id_type=MESH,
+    )
+
+
+def one_line(block):
+    return jnp.concatenate([block[i : i + 1] for i in range(block.shape[0])], axis=1)
+
+
+def fill_iota(iota_ref):
+    iota_ref[...] = lax.broadcasted_iota(jnp.int32, iota_ref.shape, 0).astype(F32).astype(BF16)
+
+
+def split_codes(s, packed):
+    count = s.inner * s.kept
+    return packed // count, packed % count
+
+
+def spread_kernel(
+    s, code_ref, psi_ref, weight_ref, got_ref, basis_ref,
+    acc, held, iota_ref, send_sem, recv_sem, own_sem, basis_send, basis_recv,
+):
+    owner_at, band_at = lax.axis_index("ga"), lax.axis_index("band")
+    meet(("ga", "band"))
+    copies = [pltpu.make_async_copy(psi_ref, basis_ref.at[band_at], own_sem.at[s.parts])]
+    for step in range(1, lax.axis_size("band")):
+        copies.append(to_peer(
+            "band", step, psi_ref, basis_ref.at[band_at],
+            basis_send.at[step - 1], basis_recv.at[step - 1],
+        ))
+    for copy in copies:
+        copy.start()
+    fill_iota(iota_ref)
+    for part in range(s.parts):
+        acc[...] = jnp.zeros_like(acc)
+
+        @pl.loop(0, s.points // s.chunk)
+        def _(step):
+            at = pl.ds(pl.multiple_of(step * s.lines, s.lines), s.lines)
+            row_code, lane_code = split_codes(s, code_ref[at, :])
+            row_code = one_line(row_code.astype(F32)).astype(BF16)
+            lane_code = one_line(lane_code.astype(F32)).astype(BF16)
+            values = [halves(one_line(psi_ref[kind, at, :])) for kind in range(2)]
+            zero = jnp.zeros((), BF16)
+            row_hot = jnp.where(iota_ref[: s.rows, :] == row_code, jnp.ones((), BF16), zero)
+            masks = [
+                iota_ref[group * s.kept : (group + 1) * s.kept, :] == lane_code
+                for group in range(part * s.groups, (part + 1) * s.groups)
+            ]
+            total = None
+            for half in range(2):
+                value = jnp.concatenate(
+                    [jnp.where(m, values[kind][half], zero) for m in masks for kind in range(2)],
+                    axis=0,
+                )
+                term = lax.dot_general(
+                    row_hot, value, (((1,), (1,)), ((), ())), preferred_element_type=F32
+                )
+                total = term if total is None else total + term
+            acc[...] += total
+
+        for outer in range(s.outer):
+            field = acc[outer * s.kept : (outer + 1) * s.kept, :]
+            both = jnp.concatenate([field, turn(field, s.kept)], axis=0)
+            result = left_mul(weight_ref[...], both)
+            for owner in range(s.owners):
+                held[part, owner, outer] = result[owner * s.block : (owner + 1) * s.block]
+        own = pltpu.make_async_copy(
+            held.at[part, owner_at], got_ref.at[part, owner_at], own_sem.at[part]
+        )
+        own.start()
+        copies.append(own)
+        for step in range(1, s.owners):
+            peer = lax.rem(owner_at + step, s.owners)
+            copy = to_peer(
+                "ga", step, held.at[part, peer], got_ref.at[part, owner_at],
+                send_sem.at[part, step - 1], recv_sem.at[part, step - 1],
             )
-            total = term if total is None else total + term
-        acc[...] += total
-
-    for outer in range(s.outer):
-        field = acc[outer * s.kept : (outer + 1) * s.kept, :]
-        both = jnp.concatenate([field, turn(field, s.kept)], axis=0)
-        result = left_mul(weight_ref[...], both)
-        for owner in range(s.owners):
-            out_ref[owner, outer] = result[owner * s.block : (owner + 1) * s.block]
-
-
-def middle_kernel(s, in_ref, pot_ref, z_in, x_in, x_out, z_out, out_ref):
+            copy.start()
+            copies.append(copy)
+    for copy in copies:
+        copy.wait()
+
+
+def middle_kernel(
+    s, in_ref, pot_ref, z_in, x_in, x_out, z_out, got_ref, held, send_sem, recv_sem, own_sem
+):
     n = s.n
     gt = s.owners * s.outer
     width = 2 * s.kept
+    at = pl.program_id(0)
+    owner_at = lax.axis_index("ga")
+
+    @pl.when(at == 0)
+    def _():
+        meet(("ga",))
+
     planes = []
     for inner in range(s.inner):
-        value = in_ref[:, :, inner * width : (inner + 1) * width].reshape(gt * ROWS, width)
+        part, start = inner // s.groups, inner % s.groups * width
+        value = in_ref[part, :, :, start : start + width].reshape(gt * ROWS, width)
         wide = right_mul(value, z_in[...])
         for kind in range(2):
             piece = wide[:, kind * n : (kind + 1) * n].reshape(gt, ROWS, n)
@@ -160,44 +246,110 @@
             )
             kinds.append(jnp.swapaxes(piece, 0, 1).reshape(gt * ROWS, n))
         narrow = right_mul(jnp.concatenate(kinds, axis=1), z_out[...])
-        out_ref[:, :, inner * width : (inner + 1) * width] = narrow.reshape(gt, ROWS, width)
-
-
-def pick_kernel(s, in_ref, code_ref, basis_ref, iota_ref, weight_ref, out_ref, over_ref, table):
+        held[at, :, :, :, inner * width : (inner + 1) * width] = narrow.reshape(
+            s.owners, s.outer, ROWS, width
+        )
+
+    def copies(chunk):
+        yield pltpu.make_async_copy(
+            held.at[chunk, owner_at], got_ref.at[chunk, owner_at], own_sem.at[chunk]
+        )
+        for step in range(1, s.owners):
+            peer = lax.rem(owner_at + step, s.owners)
+            yield to_peer(
+                "ga", step, held.at[chunk, peer], got_ref.at[chunk, owner_at],
+                send_sem.at[chunk, step - 1], recv_sem.at[chunk, step - 1],
+            )
+
+    for copy in copies(at):
+        copy.start()
+
+    @pl.when(at == s.block // ROWS - 1)
+    def _():
+        for chunk in range(s.block // ROWS):
+            for copy in copies(chunk):
+                copy.wait()
+
+
+def pick_kernel(
+    s, in_ref, code_ref, basis_ref, occupied_ref, weight_ref, out_ref,
+    table, iota_ref, sums, send_sem, recv_sem,
+):
+    owner_at = lax.axis_index("ga")
+    bands = basis_ref.shape[0]
+    meet(("ga",))
+    fill_iota(iota_ref)
     for outer in range(s.outer):
-        rows = jnp.concatenate([in_ref[owner, outer] for owner in range(s.owners)], axis=0)
+        rows = jnp.concatenate(
+            [
+                in_ref[chunk, owner, outer]
+                for owner in range(s.owners)
+                for chunk in range(s.block // ROWS)
+            ],
+            axis=0,
+        )
         both = jnp.concatenate([rows, turn(rows, s.kept)], axis=0)
         field = left_mul(weight_ref[...], both)
         high, low = halves(field.T)
         table[:, outer * s.kept : (outer + 1) * s.kept] = high
         table[:, s.rows + outer * s.kept : s.rows + (outer + 1) * s.kept] = low
-    over_ref[...] = jnp.zeros_like(over_ref)
 
     @pl.loop(0, s.points // s.chunk)
     def _(step):
-        at = pl.ds(pl.multiple_of(step * s.chunk, s.chunk), s.chunk)
-        codes = code_ref[:, at].astype(BF16)
-        one_hot = jnp.where(iota_ref[: s.rows, :] == codes[0:1], jnp.ones((), BF16), jnp.zeros((), BF16))
+        start = pl.multiple_of(step * s.lines, s.lines)
+        row_code, lane_code = split_codes(s, code_ref[pl.ds(start, s.lines), :])
+        row_code = one_line(row_code.astype(F32)).astype(BF16)
+        lane_code = one_line(lane_code)
+        one_hot = jnp.where(
+            iota_ref[...] == row_code, jnp.ones((), BF16), jnp.zeros((), BF16)
+        )
         found = jnp.dot(table[:, : s.rows], one_hot, preferred_element_type=F32) + jnp.dot(
             table[:, s.rows :], one_hot, preferred_element_type=F32
         )
-        lane = code_ref[1:2, at]
-        index = lax.broadcasted_iota(jnp.int32, (s.kept, s.chunk), 0).astype(F32)
-        sums = [None, None]
+        index = lax.broadcasted_iota(jnp.int32, (s.kept, s.chunk), 0)
+        totals = [None, None]
         for group in range(s.inner):
-            mask = index == lane - float(group * s.kept)
+            mask = index == lane_code - group * s.kept
             for kind in range(2):
-                start = (group * 2 + kind) * s.kept
-                piece = jnp.where(mask, found[start : start + s.kept], 0.0)
-                sums[kind] = piece if sums[kind] is None else sums[kind] + piece
-        real = jnp.sum(sums[0], axis=0, keepdims=True)
-        imag = jnp.sum(sums[1], axis=0, keepdims=True)
-        out_ref[0:1, at] = real
-        out_ref[1:2, at] = imag
-        left_real = basis_ref[0, :, at]
-        left_imag = basis_ref[1, :, at]
-        over_ref[0] += left_real * real + left_imag * imag
-        over_ref[1] += left_real * imag - left_imag * real
+                first = (group * 2 + kind) * s.kept
+                piece = jnp.where(mask, found[first : first + s.kept], 0.0)
+                totals[kind] = piece if totals[kind] is None else totals[kind] + piece
+        for kind in range(2):
+            line = jnp.sum(totals[kind], axis=0, keepdims=True)
+            for i in range(s.lines):
+                out_ref[kind, pl.ds(start + i, 1), :] = line[:, i * LANES : (i + 1) * LANES]
+
+    real, imag = out_ref[0], out_ref[1]
+    pieces = []
+    for band in range(bands):
+        left_real, left_imag = basis_ref[band, 0], basis_ref[band, 1]
+        pieces.append(jnp.sum(left_real * real + left_imag * imag, axis=0, keepdims=True))
+        pieces.append(jnp.sum(left_real * imag - left_imag * real, axis=0, keepdims=True))
+    sums[owner_at] = jnp.concatenate(pieces, axis=0)
+    copies = [
+        to_peer(
+            "ga", step, sums.at[owner_at], sums.at[owner_at],
+            send_sem.at[step - 1], recv_sem.at[step - 1],
+        )
+        for step in range(1, s.owners)
+    ]
+    for copy in copies:
+        copy.start()
+    for copy in copies:
+        copy.wait()
+    total = sums[0]
+    for owner in range(1, s.owners):
+        total = total + sums[owner]
+    total = jnp.sum(total, axis=1, keepdims=True) / float(s.points * s.owners)
+    for band in range(bands):
+        kept = occupied_ref[band].astype(F32)
+        over_real = total[2 * band : 2 * band + 1] * kept
+        over_imag = total[2 * band + 1 : 2 * band + 2] * kept
+        left_real, left_imag = basis_ref[band, 0], basis_ref[band, 1]
+        real = real - (left_real * over_real - left_imag * over_imag)
+        imag = imag - (left_real * over_imag + left_imag * over_real)
+    out_ref[0] = real
+    out_ref[1] = imag
 
 
 def local_codes(s, miller):
@@ -208,21 +360,18 @@
     column = (points + quarter) % s.n
     high = slot // s.inner * s.kept + row
     low = slot % s.inner * s.kept + column
-    return jnp.stack([high, low]).astype(F32)
+    return (high * (s.inner * s.kept) + low).reshape(-1, LANES)
 
 
 VMEM = pl.BlockSpec(memory_space=pltpu.VMEM)
-PARAMS = pltpu.CompilerParams(vmem_limit_bytes=56 * 1024 * 1024)
-
-
-def call(kernel, s, out, count, scratch=()):
-    return pl.pallas_call(
-        functools.partial(kernel, s),
-        out_shape=out,
-        in_specs=[VMEM] * count,
-        out_specs=jax.tree.map(lambda _: VMEM, out),
-        scratch_shapes=list(scratch),
-        compiler_params=PARAMS,
+SMEM = pl.BlockSpec(memory_space=pltpu.SMEM)
+ANY = pl.BlockSpec(memory_space=pl.ANY)
+DMA = pltpu.SemaphoreType.DMA
+
+
+def params(number):
+    return pltpu.CompilerParams(
+        vmem_limit_bytes=56 * 1024 * 1024, collective_id=number, has_side_effects=True
     )
 
 
@@ -230,41 +379,61 @@
     s = Sizes(psi, potential, lax.axis_size("ga"))
     w = twiddles(s)
     shape = jax.ShapeDtypeStruct
-    basis = lax.all_gather(psi, "band", axis=1, tiled=True)
+    bands = lax.axis_size("band")
+    peers = s.owners - 1
+    gt = s.owners * s.outer
+    chunks = s.block // ROWS
     codes = local_codes(s, miller)
-    count = max(s.rows, s.inner * s.kept)
-    iota = lax.broadcasted_iota(jnp.int32, (count, s.chunk), 0).astype(BF16)
-    sent = call(
-        spread_kernel, s, shape((s.owners, s.outer, s.block, s.lanes), F32), 4,
-        [pltpu.VMEM((s.rows, s.lanes), F32)],
-    )(codes, psi[:, 0], iota, w["rows_in"])
-    got = lax.all_to_all(sent, "ga", split_axis=0, concat_axis=0, tiled=True)
-    gt = s.owners * s.outer
+    dense = psi.reshape(2, s.points // LANES, LANES)
+    arrived = (s.parts, s.owners, s.outer, s.block, s.width)
+    got, basis = pl.pallas_call(
+        functools.partial(spread_kernel, s),
+        out_shape=(shape(arrived, F32), shape((bands,) + dense.shape, F32)),
+        in_specs=[VMEM] * 3,
+        out_specs=(ANY, ANY),
+        scratch_shapes=[
+            pltpu.VMEM((s.rows, s.width), F32),
+            pltpu.VMEM(arrived, F32),
+            pltpu.VMEM((max(s.rows, s.inner * s.kept), s.chunk), BF16),
+            DMA((s.parts, peers)), DMA((s.parts, peers)), DMA((s.parts + 1,)),
+            DMA((bands - 1,)), DMA((bands - 1,)),
+        ],
+        compiler_params=params(0),
+        name="spread",
+    )(codes, dense, w["rows_in"])
     whole = [w["z_in"], w["x_in"], w["x_out"], w["z_out"]]
-    sent = pl.pallas_call(
+    arrived = (chunks, s.owners, s.outer, ROWS, s.lanes)
+    got = pl.pallas_call(
         functools.partial(middle_kernel, s),
-        out_shape=shape((gt, s.block, s.lanes), F32),
-        grid=(s.block // ROWS,),
+        out_shape=shape(arrived, F32),
+        grid=(chunks,),
         in_specs=[
-            pl.BlockSpec((gt, ROWS, s.lanes), lambda i: (0, i, 0)),
+            pl.BlockSpec((s.parts, gt, ROWS, s.width), lambda i: (0, 0, i, 0)),
             pl.BlockSpec((s.n, ROWS, s.n), lambda i: (0, i, 0)),
         ] + [pl.BlockSpec(v.shape, lambda i: (0, 0)) for v in whole],
-        out_specs=pl.BlockSpec((gt, ROWS, s.lanes), lambda i: (0, i, 0)),
-        compiler_params=PARAMS,
-    )(got.reshape(gt, s.block, s.lanes), potential, *whole)
-    sent = sent.reshape(s.owners, s.outer, s.block, s.lanes)
-    got = lax.all_to_all(sent, "ga", split_axis=0, concat_axis=0, tiled=True)
-    bands = basis.shape[1]
-    applied, over = call(
-        pick_kernel, s, (shape((2, s.points), F32), shape((2, bands, s.chunk), F32)), 5,
-        [pltpu.VMEM((s.lanes, 2 * s.rows), BF16)],
-    )(got, codes, basis, iota, w["rows_out"])
-    total = s.points * s.owners
-    over = lax.psum(jnp.sum(over, axis=2), "ga") / total * occupied.astype(F32)
-    real, imag = over[0][:, None], over[1][:, None]
-    proj_real = jnp.sum(basis[0] * real - basis[1] * imag, axis=0)
-    proj_imag = jnp.sum(basis[0] * imag + basis[1] * real, axis=0)
-    return jnp.stack([applied[0] - proj_real, applied[1] - proj_imag])[:, None]
+        out_specs=ANY,
+        scratch_shapes=[
+            pltpu.VMEM(arrived, F32),
+            DMA((chunks, peers)), DMA((chunks, peers)), DMA((chunks,)),
+        ],
+        compiler_params=params(1),
+        name="middle",
+    )(got.reshape(s.parts, gt, s.block, s.width), potential, *whole)
+    out = pl.pallas_call(
+        functools.partial(pick_kernel, s),
+        out_shape=shape(dense.shape, F32),
+        in_specs=[VMEM, VMEM, VMEM, SMEM, VMEM],
+        out_specs=VMEM,
+        scratch_shapes=[
+            pltpu.VMEM((s.lanes, 2 * s.rows), BF16),
+            pltpu.VMEM((s.rows, s.chunk), BF16),
+            pltpu.VMEM((s.owners, 2 * bands, LANES), F32),
+            DMA((peers,)), DMA((peers,)),
+        ],
+        compiler_params=params(2),
+        name="pick",
+    )(got, codes, basis, occupied, w["rows_out"])
+    return out.reshape(psi.shape)
 
 
 highest = lax.Precision.HIGHEST

time: 155 us -> 109 us (0.70)
  waiting for transfers between devices: 48 us -> 0 us
  Pallas kernels: 57.4 us -> 105 us
  between operations: 13.5 us -> 0.03 us
  starting transfers between devices: 10 us -> 0 us
  blocking collectives: 9.82 us -> 0 us
  local copies, waits for them, and re-layouts: 9.46 us -> 1.67 us
  other arithmetic: 5.94 us -> 2.06 us
    pallas_call x3, Pallas kernels: 57.4 us -> 105 us  [the longest x1 42.3 us: shards(): pl.pallas_call(functools.partial(spread_kernel, s), out_shape=(shape(arri...]
    all_to_all x2 -> x0, waiting for transfers between devices: 47.3 us -> none  [shards(): got = lax.all_to_all(sent, 'ga', split_axis=0, concat_axis=0, tiled=True)]
    all_to_all x2 -> x0, starting transfers between devices: 9.99 us -> none  [shards(): got = lax.all_to_all(sent, 'ga', split_axis=0, concat_axis=0, tiled=True)]
    psum x1 -> x0, blocking collectives: 9.82 us -> none  [shards(): over = lax.psum(jnp.sum(over, axis=2), 'ga') / total * occupied.astype(F32)]
    all_gather x1 -> x0, local copies, waits for them, and re-layouts: 2.9 us -> none  [shards(): basis = lax.all_gather(psi, 'band', axis=1, tiled=True)]
    add x2 -> x0, other arithmetic: 2.53 us -> none  [the longest x1 1.31 us: local_codes(): high = slot // s.inner * s.kept + row]
    unnamed x13 -> x1, local copies, waits for them, and re-layouts: 3.86 us -> 1.67 us
    reshape x0 -> x1, other arithmetic: none -> 2.06 us  [local_codes(): return (high * (s.inner * s.kept) + low).reshape(-1, LANES)]
  transfers between devices with their start and end apart: 3 -> 0, of which waited for: 2 -> 0; matrix products, arithmetic and copies ran while one was open for 2% -> 0% of each run, Pallas kernels for 5% -> 0%
where the time goes in v2:
time: 109 us
  Pallas kernels  105 us (96%)
  other arithmetic  2.06 us (2%)
  local copies, waits for them, and re-layouts  1.67 us (2%)
    pallas_call x1, Pallas kernels, shards(): pl.pallas_call(functools.partial(spread_kernel, s), out_shape=(shape(arri...  42.3 us
    pallas_call x1, Pallas kernels, shards(): pl.pallas_call(functools.partial(pick_kernel, s), out_shape=shape(dense.s...  33.8 us
    pallas_call x1, Pallas kernels, shards(): pl.pallas_call(functools.partial(middle_kernel, s), out_shape=shape(arriv...  29.1 us

profile of v2, /device:TPU:0, one launch (start us, length us, event | category | flops | bytes accessed | tf_op | source)
XLA Modules:
  0.0 109.0 jit_solution(9162386755447200129)
XLA Ops:
  0.0 2.1 %fusion.8.code_ref = s32[256,128]{1,0:T(8,128)} fusion(s32[131072]{0:T(1024)} %param.12, s32[]{:T(128)S(6)} %select_n.36), kind=kLoop, calls=%fused_computation.33 | loop fusion | flops 3309568 | bytes 262148 | tf_op jit(solution)/shard_map/reshape | solution.py:363
  2.1 42.3 %spread.1 = (f32[2,4,4,32,256]{4,3,2,1,0:T(8,128)}, f32[4,2,256,128]{3,2,1,0:T(8,128)}) custom-call(s32[256,128]{1,0:T(8,128)} %fusion.8.code_ref, f32[2,256,128]{2,1,0:T(8,128)} %bitcast.7, bf16[128,384]{1,0:T(8,128)(2,1)} %constant.104.clone.weight_ref), custom_call_target="tpu_custom_call" | custom-call | tf_op jit(solution)/shard_map/spread/pallas_call | solution.py:389
  44.4 29.1 %middle.1.in_ref = f32[4,4,4,8,512]{4,3,2,1,0:T(8,128)} custom-call(f32[2,16,32,256]{3,2,1,0:T(8,128)} %bitcast.5, f32[128,32,128]{2,1,0:T(8,128)} %pot_ref.1, bf16[384,256]{1,0:T(8,128)(2,1)} %constant.106.clone.z_in, bf16[256,384]{1,0:T(8,128)(2,1)} %constant.108.clone.x_in, bf16[128,768]{1,0:T(8,128)(2,1)} %constant.109.clone.x_out, ...), custom_call_target="tpu_custom_call" | custom-call | tf_op jit(solution)/shard_map/middle/pallas_call | solution.py:406
  73.5 33.8 %pick.1 = f32[2,256,128]{2,1,0:T(8,128)} custom-call(f32[4,4,4,8,512]{4,3,2,1,0:T(8,128)} %middle.1.in_ref, s32[256,128]{1,0:T(8,128)} %fusion.8.code_ref, f32[4,2,256,128]{3,2,1,0:T(8,128)} %get-tuple-element.8.basis_ref, s32[4]{0:T(128)} %occupied_ref.1, bf16[64,768]{1,0:T(8,128)(2,1)} %constant.105.clone.weight_ref), custom_call_target="tpu_custom_call" | custom-call | tf_op jit(solution)/shard_map/pick/pallas_call | solution.py:422
  107.3 1.7 %copy.13 = f32[2,1,32768]{2,1,0:T(1,128)} copy(f32[2,1,32768]{2,1,0:T(1,128)} %bitcast.6) | data formatting | bytes 524288

commit v3 on v1

--- a/solution.py
+++ b/solution.py
@@ -11,6 +11,8 @@
 F32 = jnp.float32
 BF16 = jnp.bfloat16
 CHUNK = 2048
+LANES = 128
+MESH = pl.DeviceIdType.MESH
 ROWS = 8
 
 
@@ -67,6 +69,11 @@
         self.rows = self.outer * self.kept
         self.lanes = self.inner * 2 * self.kept
         self.chunk = min(CHUNK, self.points)
+        self.lines = self.chunk // LANES
+        self.parts = 2
+        self.groups = self.inner // self.parts
+        self.chunks = self.block // ROWS
+        self.width = self.groups * 2 * self.kept
 
 
 def twiddles(s):
@@ -100,45 +107,90 @@
     }
 
 
-def spread_kernel(s, code_ref, psi_ref, iota_ref, weight_ref, out_ref, acc):
+def meet(axes):
+    barrier = pltpu.get_barrier_semaphore()
+    for axis in axes:
+        size = lax.axis_size(axis)
+        for step in range(1, size):
+            peer = lax.rem(lax.axis_index(axis) + step, size)
+            pl.semaphore_signal(barrier, inc=1, device_id={axis: peer}, device_id_type=MESH)
+    pl.semaphore_wait(barrier, sum(lax.axis_size(axis) - 1 for axis in axes))
+
+
+def to_peer(axis, step, source, target, send_sem, recv_sem):
+    size = lax.axis_size(axis)
+    peer = lax.rem(lax.axis_index(axis) + step, size)
+    return pltpu.make_async_remote_copy(
+        src_ref=source,
+        dst_ref=target,
+        send_sem=send_sem,
+        recv_sem=recv_sem,
+        device_id={axis: peer},
+        device_id_type=MESH,
+    )
+
+
+def one_line(block):
+    return jnp.concatenate([block[i : i + 1] for i in range(block.shape[0])], axis=1)
+
+
+def fill_iota(iota_ref):
+    iota_ref[...] = lax.broadcasted_iota(jnp.int32, iota_ref.shape, 0).astype(F32).astype(BF16)
+
+
+def log2(value):
+    return value.bit_length() - 1
+
+
+def find_codes(s, points):
+    n, quarter = s.n, s.n // 4
+    plane = lax.shift_right_logical(points, 2 * log2(n)) + quarter & n - 1
+    slot = lax.shift_right_logical(plane, log2(s.owners))
+    row = lax.shift_right_logical(points, log2(n)) + quarter & n - 1
+    column = points + quarter & n - 1
+    outer = lax.shift_right_logical(slot, log2(s.inner))
+    return outer * s.kept + row, (slot & s.inner - 1) * s.kept + column
+
+
+def scatter(s, part, codes, psi_ref, iota_ref, acc):
     acc[...] = jnp.zeros_like(acc)
 
     @pl.loop(0, s.points // s.chunk)
     def _(step):
-        at = pl.ds(pl.multiple_of(step * s.chunk, s.chunk), s.chunk)
-        codes = code_ref[:, at].astype(BF16)
-        high, low = halves(psi_ref[:, at])
+        at = pl.ds(pl.multiple_of(step * s.lines, s.lines), s.lines)
+        row_code = one_line(codes[0, at, :].astype(F32)).astype(BF16)
+        lane_code = codes[1, at, :] - part * (s.groups * s.kept)
+        lane_code = one_line(lane_code.astype(F32)).astype(BF16)
+        values = [halves(one_line(psi_ref[kind, at, :])) for kind in range(2)]
         zero = jnp.zeros((), BF16)
-        row_hot = jnp.where(iota_ref[: s.rows, :] == codes[0:1], jnp.ones((), BF16), zero)
+        row_hot = jnp.where(iota_ref[: s.rows, :] == row_code, jnp.ones((), BF16), zero)
+        masks = [
+            iota_ref[group * s.kept : (group + 1) * s.kept, :] == lane_code
+            for group in range(s.groups)
+        ]
         total = None
-        for part in (high, low):
-            pieces = []
-            for group in range(s.inner):
-                mask = iota_ref[group * s.kept : (group + 1) * s.kept, :] == codes[1:2]
-                for kind in range(2):
-                    pieces.append(jnp.where(mask, part[kind : kind + 1], zero))
-            value = jnp.concatenate(pieces, axis=0)
+        for half in range(2):
+            value = jnp.concatenate(
+                [jnp.where(m, values[kind][half], zero) for m in masks for kind in range(2)],
+                axis=0,
+            )
             term = lax.dot_general(
                 row_hot, value, (((1,), (1,)), ((), ())), preferred_element_type=F32
             )
             total = term if total is None else total + term
         acc[...] += total
 
-    for outer in range(s.outer):
-        field = acc[outer * s.kept : (outer + 1) * s.kept, :]
-        both = jnp.concatenate([field, turn(field, s.kept)], axis=0)
-        result = left_mul(weight_ref[...], both)
-        for owner in range(s.owners):
-            out_ref[owner, outer] = result[owner * s.block : (owner + 1) * s.block]
-
-
-def middle_kernel(s, in_ref, pot_ref, z_in, x_in, x_out, z_out, out_ref):
+
+def apply_rows(s, at, landed, pot_vmem, weights, held):
+    z_in, x_in, x_out, z_out = weights
     n = s.n
     gt = s.owners * s.outer
     width = 2 * s.kept
+    rows_at = pl.ds(pl.multiple_of(at * ROWS, ROWS), ROWS)
     planes = []
     for inner in range(s.inner):
-        value = in_ref[:, :, inner * width : (inner + 1) * width].reshape(gt * ROWS, width)
+        part, start = inner // s.groups, inner % s.groups * width
+        value = landed[part, :, :, rows_at, start : start + width].reshape(gt * ROWS, width)
         wide = right_mul(value, z_in[...])
         for kind in range(2):
             piece = wide[:, kind * n : (kind + 1) * n].reshape(gt, ROWS, n)
@@ -147,11 +199,12 @@
         jnp.concatenate([piece[row] for piece in planes], axis=0) for row in range(ROWS)
     ]
     wave = left_mul(x_in[...], jnp.concatenate(columns, axis=1))
-    pot = jnp.swapaxes(pot_ref[...], 0, 1)
+    pot = jnp.swapaxes(pot_vmem[:, rows_at, :], 0, 1)
     pot = jnp.concatenate([pot[row] for row in range(ROWS)], axis=1)
     product = jnp.concatenate([wave[:n] * pot, wave[n:] * pot], axis=0)
     back = left_mul(x_out[...], product)
     for inner in range(s.inner):
+        part, first = inner // s.groups, inner % s.groups * width
         kinds = []
         for kind in range(2):
             start = (inner * 2 + kind) * gt
@@ -160,111 +213,260 @@
             )
             kinds.append(jnp.swapaxes(piece, 0, 1).reshape(gt * ROWS, n))
         narrow = right_mul(jnp.concatenate(kinds, axis=1), z_out[...])
-        out_ref[:, :, inner * width : (inner + 1) * width] = narrow.reshape(gt, ROWS, width)
-
-
-def pick_kernel(s, in_ref, code_ref, basis_ref, iota_ref, weight_ref, out_ref, over_ref, table):
-    for outer in range(s.outer):
-        rows = jnp.concatenate([in_ref[owner, outer] for owner in range(s.owners)], axis=0)
-        both = jnp.concatenate([rows, turn(rows, s.kept)], axis=0)
-        field = left_mul(weight_ref[...], both)
-        high, low = halves(field.T)
-        table[:, outer * s.kept : (outer + 1) * s.kept] = high
-        table[:, s.rows + outer * s.kept : s.rows + (outer + 1) * s.kept] = low
-    over_ref[...] = jnp.zeros_like(over_ref)
-
+        held[part, :, at, :, :, first : first + width] = narrow.reshape(
+            s.owners, s.outer, ROWS, width
+        )
+
+
+def gather(s, part, codes, iota_ref, table, out_ref):
     @pl.loop(0, s.points // s.chunk)
     def _(step):
-        at = pl.ds(pl.multiple_of(step * s.chunk, s.chunk), s.chunk)
-        codes = code_ref[:, at].astype(BF16)
-        one_hot = jnp.where(iota_ref[: s.rows, :] == codes[0:1], jnp.ones((), BF16), jnp.zeros((), BF16))
-        found = jnp.dot(table[:, : s.rows], one_hot, preferred_element_type=F32) + jnp.dot(
-            table[:, s.rows :], one_hot, preferred_element_type=F32
-        )
-        lane = code_ref[1:2, at]
-        index = lax.broadcasted_iota(jnp.int32, (s.kept, s.chunk), 0).astype(F32)
-        sums = [None, None]
-        for group in range(s.inner):
-            mask = index == lane - float(group * s.kept)
+        start = pl.multiple_of(step * s.lines, s.lines)
+        at = pl.ds(start, s.lines)
+        row_code = one_line(codes[0, at, :].astype(F32)).astype(BF16)
+        lane_code = one_line(codes[1, at, :])
+        one_hot = jnp.where(
+            iota_ref[: s.rows, :] == row_code, jnp.ones((), BF16), jnp.zeros((), BF16)
+        )
+        found = jnp.dot(
+            table[...], jnp.concatenate([one_hot, one_hot], axis=0), preferred_element_type=F32
+        )
+        index = lax.broadcasted_iota(jnp.int32, (s.kept, s.chunk), 0)
+        totals = [None, None]
+        for group in range(s.groups):
+            mask = index == lane_code - (part * s.groups + group) * s.kept
             for kind in range(2):
-                start = (group * 2 + kind) * s.kept
-                piece = jnp.where(mask, found[start : start + s.kept], 0.0)
-                sums[kind] = piece if sums[kind] is None else sums[kind] + piece
-        real = jnp.sum(sums[0], axis=0, keepdims=True)
-        imag = jnp.sum(sums[1], axis=0, keepdims=True)
-        out_ref[0:1, at] = real
-        out_ref[1:2, at] = imag
-        left_real = basis_ref[0, :, at]
-        left_imag = basis_ref[1, :, at]
-        over_ref[0] += left_real * real + left_imag * imag
-        over_ref[1] += left_real * imag - left_imag * real
-
-
-def local_codes(s, miller):
-    quarter = s.n // 4
-    points = lax.dynamic_slice_in_dim(miller, lax.axis_index("ga") * s.points, s.points)
-    slot = (points // (s.n * s.n) + quarter) % s.n // s.owners
-    row = (points // s.n + quarter) % s.n
-    column = (points + quarter) % s.n
-    high = slot // s.inner * s.kept + row
-    low = slot % s.inner * s.kept + column
-    return jnp.stack([high, low]).astype(F32)
+                first = (group * 2 + kind) * s.kept
+                piece = jnp.where(mask, found[first : first + s.kept], 0.0)
+                totals[kind] = piece if totals[kind] is None else totals[kind] + piece
+        for kind in range(2):
+            line = jnp.sum(totals[kind], axis=0, keepdims=True)
+            for i in range(s.lines):
+                value = line[:, i * LANES : (i + 1) * LANES]
+                if part:
+                    value = value + out_ref[kind, pl.ds(start + i, 1), :]
+                out_ref[kind, pl.ds(start + i, 1), :] = value
+
+
+def whole_kernel(
+    s, miller_ref, psi_ref, pot_ref, occupied_ref,
+    rows_in, z_in, x_in, x_out, z_out, rows_out, out_ref,
+    points, codes, basis, pot_vmem, iota_ref, acc, held, landed, back_held, back_landed,
+    table, sums, local_sem, basis_send, basis_recv, send_sem, recv_sem, swap_send, swap_recv,
+    first_send, first_recv, first_own, back_send, back_recv, back_own, sum_send, sum_recv,
+):
+    owner_at, band_at = lax.axis_index("ga"), lax.axis_index("band")
+    part_at = lax.axis_index("pert")
+    lines = s.points // LANES
+    bands = basis.shape[0]
+    sources = [lax.rem(owner_at + s.owners - step, s.owners) for step in range(s.owners)]
+    targets = [lax.rem(owner_at + step, s.owners) for step in range(s.owners)]
+    find = pltpu.make_async_copy(
+        miller_ref.at[pl.ds(pl.multiple_of(owner_at * lines, lines), lines), :],
+        points, local_sem.at[0],
+    )
+    find.start()
+    fetch = pltpu.make_async_copy(pot_ref, pot_vmem, local_sem.at[1])
+    fetch.start()
+    keep = pltpu.make_async_copy(psi_ref, basis.at[band_at], local_sem.at[2])
+    keep.start()
+    meet(("ga", "band", "pert"))
+    spread = [
+        to_peer(
+            "band", step, psi_ref, basis.at[band_at],
+            basis_send.at[step - 1], basis_recv.at[step - 1],
+        )
+        for step in range(1, bands)
+    ]
+    for copy in spread:
+        copy.start()
+    fill_iota(iota_ref)
+    find.wait()
+    row_code, lane_code = find_codes(s, points[...])
+    codes[0] = row_code
+    codes[1] = lane_code
+    scatter(s, part_at, codes, psi_ref, iota_ref, acc)
+    for outer in range(s.outer):
+        field = acc[outer * s.kept : (outer + 1) * s.kept, :]
+        both = jnp.concatenate([field, turn(field, s.kept)], axis=0)
+        result = left_mul(rows_in[...], both)
+        for owner in range(s.owners):
+            held[owner, outer] = result[owner * s.block : (owner + 1) * s.block]
+    out = [
+        to_peer(
+            "ga", step, held.at[targets[step]], landed.at[part_at, owner_at],
+            send_sem.at[step - 1], recv_sem.at[step - 1],
+        )
+        for step in range(1, s.owners)
+    ]
+    for copy in out:
+        copy.start()
+    own = pltpu.make_async_copy(held.at[owner_at], landed.at[part_at, owner_at], local_sem.at[3])
+    own.start()
+    swaps = []
+    for step in range(s.owners):
+        if step:
+            out[step - 1].wait_recv()
+            source = landed.at[part_at, sources[step]]
+        else:
+            source = held.at[owner_at]
+        swap = to_peer(
+            "pert", 1, source, landed.at[part_at, sources[step]],
+            swap_send.at[step], swap_recv.at[step],
+        )
+        swap.start()
+        swaps.append(swap)
+    fetch.wait()
+    own.wait()
+    for swap in swaps:
+        swap.wait_recv()
+
+    weights = (z_in, x_in, x_out, z_out)
+
+    def early(at, step):
+        return to_peer(
+            "ga", step, back_held.at[0, targets[step], at], back_landed.at[0, owner_at, at],
+            first_send.at[at, step - 1], first_recv.at[at, step - 1],
+        )
+
+    @pl.loop(0, s.chunks)
+    def _(at):
+        apply_rows(s, at, landed, pot_vmem, weights, back_held)
+        for step in range(1, s.owners):
+            early(at, step).start()
+
+    late = [
+        to_peer(
+            "ga", step, back_held.at[1, targets[step]], back_landed.at[1, owner_at],
+            back_send.at[step - 1], back_recv.at[step - 1],
+        )
+        for step in range(1, s.owners)
+    ]
+    for copy in late:
+        copy.start()
+    mine = [
+        pltpu.make_async_copy(
+            back_held.at[part, owner_at], back_landed.at[part, owner_at], back_own.at[part]
+        )
+        for part in range(s.parts)
+    ]
+    for copy in mine:
+        copy.start()
+    for part in range(s.parts):
+        mine[part].wait()
+        if part == 0:
+            for at in range(s.chunks):
+                for step in range(1, s.owners):
+                    early(at, step).wait_recv()
+        else:
+            for copy in late:
+                copy.wait_recv()
+        for outer in range(s.outer):
+            rows = jnp.concatenate(
+                [
+                    back_landed[part, owner, at, outer]
+                    for owner in range(s.owners)
+                    for at in range(s.chunks)
+                ],
+                axis=0,
+            )
+            both = jnp.concatenate([rows, turn(rows, s.kept)], axis=0)
+            high, low = halves(left_mul(rows_out[...], both).T)
+            table[:, outer * s.kept : (outer + 1) * s.kept] = high
+            table[:, s.rows + outer * s.kept : s.rows + (outer + 1) * s.kept] = low
+        gather(s, part, codes, iota_ref, table, out_ref)
+
+    keep.wait()
+    for copy in spread:
+        copy.wait_recv()
+    real, imag = out_ref[0], out_ref[1]
+    pieces = []
+    for band in range(bands):
+        left_real, left_imag = basis[band, 0], basis[band, 1]
+        pieces.append(jnp.sum(left_real * real + left_imag * imag, axis=0, keepdims=True))
+        pieces.append(jnp.sum(left_real * imag - left_imag * real, axis=0, keepdims=True))
+    sums[owner_at] = jnp.concatenate(pieces, axis=0)
+    adds = [
+        to_peer(
+            "ga", step, sums.at[owner_at], sums.at[owner_at],
+            sum_send.at[step - 1], sum_recv.at[step - 1],
+        )
+        for step in range(1, s.owners)
+    ]
+    for copy in adds:
+        copy.start()
+    for copy in adds:
+        copy.wait_recv()
+    total = sums[0]
+    for owner in range(1, s.owners):
+        total = total + sums[owner]
+    total = jnp.sum(total, axis=1, keepdims=True) / float(s.points * s.owners)
+    for band in range(bands):
+        kept = occupied_ref[band].astype(F32)
+        over_real = total[2 * band : 2 * band + 1] * kept
+        over_imag = total[2 * band + 1 : 2 * band + 2] * kept
+        left_real, left_imag = basis[band, 0], basis[band, 1]
+        real = real - (left_real * over_real - left_imag * over_imag)
+        imag = imag - (left_real * over_imag + left_imag * over_real)
+    out_ref[0] = real
+    out_ref[1] = imag
+    for at in range(s.chunks):
+        for step in range(1, s.owners):
+            early(at, step).wait_send()
+    for copy in spread + out + swaps + late + adds:
+        copy.wait_send()
 
 
 VMEM = pl.BlockSpec(memory_space=pltpu.VMEM)
-PARAMS = pltpu.CompilerParams(vmem_limit_bytes=56 * 1024 * 1024)
-
-
-def call(kernel, s, out, count, scratch=()):
-    return pl.pallas_call(
-        functools.partial(kernel, s),
-        out_shape=out,
-        in_specs=[VMEM] * count,
-        out_specs=jax.tree.map(lambda _: VMEM, out),
-        scratch_shapes=list(scratch),
-        compiler_params=PARAMS,
-    )
+SMEM = pl.BlockSpec(memory_space=pltpu.SMEM)
+ANY = pl.BlockSpec(memory_space=pl.ANY)
+DMA = pltpu.SemaphoreType.DMA
 
 
 def shards(psi, potential, miller, occupied):
     s = Sizes(psi, potential, lax.axis_size("ga"))
     w = twiddles(s)
-    shape = jax.ShapeDtypeStruct
-    basis = lax.all_gather(psi, "band", axis=1, tiled=True)
-    codes = local_codes(s, miller)
-    count = max(s.rows, s.inner * s.kept)
-    iota = lax.broadcasted_iota(jnp.int32, (count, s.chunk), 0).astype(BF16)
-    sent = call(
-        spread_kernel, s, shape((s.owners, s.outer, s.block, s.lanes), F32), 4,
-        [pltpu.VMEM((s.rows, s.lanes), F32)],
-    )(codes, psi[:, 0], iota, w["rows_in"])
-    got = lax.all_to_all(sent, "ga", split_axis=0, concat_axis=0, tiled=True)
-    gt = s.owners * s.outer
-    whole = [w["z_in"], w["x_in"], w["x_out"], w["z_out"]]
-    sent = pl.pallas_call(
-        functools.partial(middle_kernel, s),
-        out_shape=shape((gt, s.block, s.lanes), F32),
-        grid=(s.block // ROWS,),
-        in_specs=[
-            pl.BlockSpec((gt, ROWS, s.lanes), lambda i: (0, i, 0)),
-            pl.BlockSpec((s.n, ROWS, s.n), lambda i: (0, i, 0)),
-        ] + [pl.BlockSpec(v.shape, lambda i: (0, 0)) for v in whole],
-        out_specs=pl.BlockSpec((gt, ROWS, s.lanes), lambda i: (0, i, 0)),
-        compiler_params=PARAMS,
-    )(got.reshape(gt, s.block, s.lanes), potential, *whole)
-    sent = sent.reshape(s.owners, s.outer, s.block, s.lanes)
-    got = lax.all_to_all(sent, "ga", split_axis=0, concat_axis=0, tiled=True)
-    bands = basis.shape[1]
-    applied, over = call(
-        pick_kernel, s, (shape((2, s.points), F32), shape((2, bands, s.chunk), F32)), 5,
-        [pltpu.VMEM((s.lanes, 2 * s.rows), BF16)],
-    )(got, codes, basis, iota, w["rows_out"])
-    total = s.points * s.owners
-    over = lax.psum(jnp.sum(over, axis=2), "ga") / total * occupied.astype(F32)
-    real, imag = over[0][:, None], over[1][:, None]
-    proj_real = jnp.sum(basis[0] * real - basis[1] * imag, axis=0)
-    proj_imag = jnp.sum(basis[0] * imag + basis[1] * real, axis=0)
-    return jnp.stack([applied[0] - proj_real, applied[1] - proj_imag])[:, None]
+    bands = lax.axis_size("band")
+    peers = s.owners - 1
+    lines = s.points // LANES
+    dense = (2, lines, LANES)
+    names = ("rows_in", "z_in", "x_in", "x_out", "z_out", "rows_out")
+    back = (s.parts, s.owners, s.chunks, s.outer, ROWS, s.width)
+    out = pl.pallas_call(
+        functools.partial(whole_kernel, s),
+        out_shape=jax.ShapeDtypeStruct(dense, F32),
+        in_specs=[ANY, VMEM, ANY, SMEM] + [VMEM] * len(names),
+        out_specs=VMEM,
+        scratch_shapes=[
+            pltpu.VMEM((lines, LANES), jnp.int32),
+            pltpu.VMEM(dense, jnp.int32),
+            pltpu.VMEM((bands,) + dense, F32),
+            pltpu.VMEM(potential.shape, F32),
+            pltpu.VMEM((max(s.rows, s.groups * s.kept), s.chunk), BF16),
+            pltpu.VMEM((s.rows, s.width), F32),
+            pltpu.VMEM((s.owners, s.outer, s.block, s.width), F32),
+            pltpu.VMEM((s.parts, s.owners, s.outer, s.block, s.width), F32),
+            pltpu.VMEM(back, F32),
+            pltpu.VMEM(back, F32),
+            pltpu.VMEM((s.width, 2 * s.rows), BF16),
+            pltpu.VMEM((s.owners, 2 * bands, LANES), F32),
+            DMA((4,)),
+            DMA((bands - 1,)), DMA((bands - 1,)),
+            DMA((peers,)), DMA((peers,)),
+            DMA((s.owners,)), DMA((s.owners,)),
+            DMA((s.chunks, peers)), DMA((s.chunks, peers)), DMA((s.chunks,)),
+            DMA((peers,)), DMA((peers,)), DMA((s.parts,)),
+            DMA((peers,)), DMA((peers,)),
+        ],
+        compiler_params=pltpu.CompilerParams(
+            vmem_limit_bytes=56 * 1024 * 1024, collective_id=0, has_side_effects=True
+        ),
+        name="whole",
+    )(
+        miller.reshape(-1, LANES), psi.reshape(dense), potential, occupied,
+        *[w[name] for name in names],
+    )
+    return out.reshape(psi.shape)
 
 
 highest = lax.Precision.HIGHEST
@@ -382,7 +584,7 @@
 
 def solution(mesh):
     def body(psi, potential, miller, occupied):
-        if potential.shape[1] % ROWS:
+        if potential.shape[1] % ROWS or lax.axis_size("pert") != 2:
             return plain_shards(psi, potential, miller, occupied)
         return shards(psi, potential, miller, occupied)
 

time: 155 us -> 94.3 us (0.61)
  waiting for transfers between devices: 48 us -> 0 us
  Pallas kernels: 57.4 us -> 92.4 us
  between operations: 13.5 us -> 0.01 us
  starting transfers between devices: 10 us -> 0 us
  blocking collectives: 9.82 us -> 0 us
  local copies, waits for them, and re-layouts: 9.46 us -> 1.67 us
  other arithmetic: 5.94 us -> 0 us
    all_to_all x2 -> x0, waiting for transfers between devices: 47.3 us -> none  [shards(): got = lax.all_to_all(sent, 'ga', split_axis=0, concat_axis=0, tiled=True)]
    pallas_call x3 -> x1, Pallas kernels: 57.4 us -> 92.4 us  [shards(): pl.pallas_call(functools.partial(whole_kernel, s), out_shape=jax.ShapeDty...]
    all_to_all x2 -> x0, starting transfers between devices: 9.99 us -> none  [shards(): got = lax.all_to_all(sent, 'ga', split_axis=0, concat_axis=0, tiled=True)]
    psum x1 -> x0, blocking collectives: 9.82 us -> none  [shards(): over = lax.psum(jnp.sum(over, axis=2), 'ga') / total * occupied.astype(F32)]
    all_gather x1 -> x0, local copies, waits for them, and re-layouts: 2.9 us -> none  [shards(): basis = lax.all_gather(psi, 'band', axis=1, tiled=True)]
    add x2 -> x0, other arithmetic: 2.53 us -> none  [the longest x1 1.31 us: local_codes(): high = slot // s.inner * s.kept + row]
    unnamed x13 -> x1, local copies, waits for them, and re-layouts: 3.86 us -> 1.67 us
    reduce_sum x2 -> x0, other arithmetic: 1.93 us -> none  [the longest x1 0.98 us: shards(): over = lax.psum(jnp.sum(over, axis=2), 'ga') / total * occupied.astype(F32)]
  transfers between devices with their start and end apart: 3 -> 0, of which waited for: 2 -> 0; matrix products, arithmetic and copies ran while one was open for 2% -> 0% of each run, Pallas kernels for 5% -> 0%
where the time goes in v3:
time: 94.3 us; the launch traced here: 94.1 us
  Pallas kernels  92.4 us (98%)
  local copies, waits for them, and re-layouts  1.67 us (2%)
    pallas_call x1, Pallas kernels, shards(): pl.pallas_call(functools.partial(whole_kernel, s), out_shape=jax.ShapeDty...  92.4 us

profile of v3, /device:TPU:0, one launch (start us, length us, event | category | flops | bytes accessed | tf_op | source)
XLA Modules:
  0.0 94.1 jit_solution(3199522157213420760)
XLA Ops:
  0.0 92.4 %whole.1 = f32[2,256,128]{2,1,0:T(8,128)} custom-call(s32[1024,128]{1,0:T(8,128)} %bitcast.4, f32[2,256,128]{2,1,0:T(8,128)} %bitcast.5, f32[128,32,128]{2,1,0:T(8,128)} %pot_ref.1, s32[4]{0:T(128)} %occupied_ref.1, bf16[128,384]{1,0:T(8,128)(2,1)} %constant.12.clone.rows_in, bf16[384,256]{1,0:T(8,128)(2,1)} %constant.14.clone.z_in, ...), custom_call_target="tpu_custom_call" | custom-call | tf_op jit(solution)/shard_map/whole/pallas_call | solution.py:435
  92.4 1.7 %copy.13 = f32[2,1,32768]{2,1,0:T(1,128)} copy(f32[2,1,32768]{2,1,0:T(1,128)} %bitcast.3) | data formatting | bytes 524288

commit v4 on v3

--- a/solution.py
+++ b/solution.py
@@ -10,7 +10,7 @@
 
 F32 = jnp.float32
 BF16 = jnp.bfloat16
-CHUNK = 2048
+CHUNK = 8192
 LANES = 128
 MESH = pl.DeviceIdType.MESH
 ROWS = 8

time: 94.3 us -> 87.7 us (0.930)
  Pallas kernels: 92.4 us -> 85.9 us
    pallas_call x1, Pallas kernels: 92.4 us -> 85.9 us  [shards(): pl.pallas_call(functools.partial(whole_kernel, s), out_shape=jax.ShapeDty...]
where the time goes in v4:
time: 87.7 us; the launch traced here: 87.6 us
  Pallas kernels  85.9 us (98%)
  local copies, waits for them, and re-layouts  1.67 us (2%)
    pallas_call x1, Pallas kernels, shards(): pl.pallas_call(functools.partial(whole_kernel, s), out_shape=jax.ShapeDty...  85.9 us

profile of v4, /device:TPU:0, one launch (start us, length us, event | category | flops | bytes accessed | tf_op | source)
XLA Modules:
  0.0 87.6 jit_solution(14211324278644583823)
XLA Ops:
  0.0 85.9 %whole.1 = f32[2,256,128]{2,1,0:T(8,128)} custom-call(s32[1024,128]{1,0:T(8,128)} %bitcast.4, f32[2,256,128]{2,1,0:T(8,128)} %bitcast.5, f32[128,32,128]{2,1,0:T(8,128)} %pot_ref.1, s32[4]{0:T(128)} %occupied_ref.1, bf16[128,384]{1,0:T(8,128)(2,1)} %constant.12.clone.rows_in, bf16[384,256]{1,0:T(8,128)(2,1)} %constant.14.clone.z_in, ...), custom_call_target="tpu_custom_call" | custom-call | tf_op jit(solution)/shard_map/whole/pallas_call | solution.py:435
  85.9 1.7 %copy.13 = f32[2,1,32768]{2,1,0:T(1,128)} copy(f32[2,1,32768]{2,1,0:T(1,128)} %bitcast.3) | data formatting | bytes 524288
